TPU v7x, 512 devices: a whole 4x8x8 slice. The times are simulated.
512 devices in a mesh: head: 8 (over z), blk: 64 (over x, y, core).
Axes of the slice: x: 4, y: 8, z: 8, core: 2. Of those that a mesh axis runs over, the one named last changes fastest.
Arguments:
- vision: bfloat16 [4, 1408, 8192], P(None, 'head', 'blk'), may hold values from -600 to 600
- ln_gain: float32 [1408], P('head'), may hold values from 0.5 to 1.5
- merge_proj: bfloat16 [4, 1408, 1408], P(None, 'head'), may hold values from -0.078125 to 0.078125
- image_slot: int32 [2048], P('blk'), may hold values from 0 to 32764, as said below
- text: bfloat16 [1408, 32768], P('head', 'blk'), may hold values from -600 to 600
- rms_gain: float32 [1408], replicated, may hold values from 0.5 to 1.5
- wqkv: bfloat16 [3, 1408, 1408], P(None, 'head'), may hold values from -0.31835938 to 0.31835938
- pcache: bfloat16 [2, 1408, 131072], P(None, 'head', 'blk'), may hold values from -300 to 300
- block_table: int32 [64, 128], replicated, may hold values from -1 to 4095, as said below
- cache_len: int32 [64], P('blk'), may hold values from 1 to 4096, as said below
Outputs:
- attended: bfloat16 [1408, 32768], P('head', 'blk')
- new_cache: bfloat16 [2, 1408, 32768], P(None, 'head', 'blk')
Inputs may be any that keep to these rules, and one draw needn't show every extreme that they name: `image_slot`: pieces never intersect and start at multiples of 4; the 32 pieces held by one index of blk start in the rows of 32 different requests, and every request receives exactly 32 pieces. `block_table`: row r holds a block number for j < ceil(cache_len[r] / 32) and -1 after; no block number appears twice; index d of blk holds blocks d * 64 to (d+1) * 64 - 1. The longest request has exactly 2 blocks on every index of blk; every other request has at most one block on any index. `cache_len`: exactly one request, the longest, has 4096 cached positions; all others have fewer.
All inputs are finite; a program needn't handle non-finite values.
Results may differ from a plain program's by a relative error of at most 0.025.
The roundings to bfloat16 on the way count: a program that leaves them out, or rounds other values in their place, can miss the bound.
Values may be sent and summed in bfloat16 or wider, within the bound.
A program may use at most 128 MiB of HBM per device.

v0:
```python
import math

import jax
import jax.numpy as jnp
from jax import lax
from jax.sharding import PartitionSpec as P

D = 1408
HD = 88
BS = 32


masked_score = -1e30


def rotary_columns(values, places):
    half = values.shape[1] // 2
    freq_index = jnp.arange(half, dtype=jnp.float32)
    inverse = jnp.exp(freq_index * (-2.0 * math.log(10000.0) / values.shape[1]))
    angles = inverse[:, None] * places[None, :]
    cosine = jnp.cos(angles)[None]
    sine_part = jnp.sin(angles)[None]
    leading = values[:, :half]
    trailing = values[:, half:]
    return jnp.concatenate(
        [leading * cosine - trailing * sine_part, trailing * cosine + leading * sine_part], axis=1
    )


def softmax_part(query_block, keys, values, mask, scale):
    scores = (
        jnp.einsum("hdq,hdk->hqk", query_block, keys, preferred_element_type=jnp.float32) * scale
    )
    scores = jnp.where(mask[None], scores, masked_score)
    highest = jnp.max(scores, axis=2)
    expo = jnp.where(mask[None], jnp.exp(scores - highest[:, :, None]), 0.0)
    total = jnp.sum(expo, axis=2)
    mixed = jnp.einsum("hqk,hdk->hdq", expo, values, precision=lax.Precision.HIGHEST)
    return (mixed, highest, total)


def fold_softmax(first, second):
    mixed_a, high_a, total_a = first
    mixed_b, high_b, total_b = second
    top = jnp.maximum(high_a, high_b)
    factor_a = jnp.exp(high_a - top)
    factor_b = jnp.exp(high_b - top)
    return (
        mixed_a * factor_a[:, None, :] + mixed_b * factor_b[:, None, :],
        top,
        total_a * factor_a + total_b * factor_b,
    )


def unblock(parts):
    mixed, highest, total = parts
    heads_here = mixed.shape[1]
    mixed = jnp.transpose(mixed, (1, 2, 0, 3)).reshape(heads_here, mixed.shape[2], -1)
    highest = jnp.transpose(highest, (1, 0, 2)).reshape(heads_here, -1)
    total = jnp.transpose(total, (1, 0, 2)).reshape(heads_here, -1)
    return (mixed, highest, total)


def shards(
    vision, ln_gain, merge_proj, image_slot, text, rms_gain, wqkv, pcache, block_table, cache_len
):
    local = vision.shape[1]
    groups = vision.shape[2]
    floats = vision.astype(jnp.float32)
    totals, squares = lax.psum((jnp.sum(floats, axis=1), jnp.sum(floats * floats, axis=1)), "head")
    average = totals / D
    spread = squares / D - average * average
    normed_vision = (
        (floats - average[:, None, :])
        * lax.rsqrt(spread + 1e-06)[:, None, :]
        * ln_gain[None, :, None]
    ).astype(jnp.bfloat16)
    partial_rows = jnp.einsum(
        "tcd,tcg->dg", merge_proj, normed_vision, preferred_element_type=jnp.float32
    )
    merged_columns = lax.psum_scatter(partial_rows, "head", scatter_dimension=0, tiled=True).astype(
        jnp.bfloat16
    )
    merged = jnp.transpose(merged_columns)
    devices = lax.axis_size("blk")
    here = lax.axis_index("blk")
    rows_here = text.shape[1]
    pieces = image_slot.shape[0]
    piece_rows = groups // pieces
    lines = jnp.arange(rows_here, dtype=jnp.int32)
    offsets = jnp.arange(piece_rows, dtype=jnp.int32)
    target = image_slot // rows_here
    within = image_slot % rows_here
    select = target[None, :] == jnp.arange(devices, dtype=jnp.int32)[:, None]
    outbound = (
        jnp.dot(
            select.astype(jnp.bfloat16),
            merged.reshape(pieces, piece_rows * local),
            preferred_element_type=jnp.float32,
        )
        .astype(jnp.bfloat16)
        .reshape(devices, piece_rows, local)
    )
    starts = jnp.sum(jnp.where(select, within[None, :] + 1, 0), axis=1) - 1
    arrived, arrived_start = (
        lax.all_to_all(outbound, "blk", split_axis=0, concat_axis=0, tiled=True),
        lax.all_to_all(starts, "blk", split_axis=0, concat_axis=0, tiled=True),
    )
    row_ids = (arrived_start[:, None] + offsets[None, :]).reshape(-1)
    present = jnp.repeat(arrived_start >= 0, piece_rows)
    hits = (row_ids[:, None] == lines[None, :]) & present[:, None]
    placed_rows = jnp.einsum(
        "kl,kr->lr",
        arrived.reshape(devices * piece_rows, local),
        hits.astype(jnp.bfloat16),
        preferred_element_type=jnp.float32,
    ).astype(jnp.bfloat16)
    covered = jnp.any(hits, axis=0)
    placed = jnp.where(covered[None, :], placed_rows, text)
    row_floats = placed.astype(jnp.float32)
    square_sums = lax.psum(jnp.sum(row_floats * row_floats, axis=0), "head")
    gain_here = lax.dynamic_slice_in_dim(rms_gain, lax.axis_index("head") * local, local)
    normed = (row_floats * lax.rsqrt(square_sums / D + 1e-06)[None, :] * gain_here[:, None]).astype(
        jnp.bfloat16
    )
    projected = jnp.einsum(
        "jod,dr->jor",
        wqkv,
        lax.all_gather(normed, "head", axis=0, tiled=True),
        preferred_element_type=jnp.float32,
    )
    heads_here = local // HD
    projected = projected.reshape(3, heads_here, HD, rows_here)
    places = (cache_len[0] + lines).astype(jnp.float32)
    queries = rotary_columns(projected[0], places).astype(jnp.bfloat16)
    new_keys = rotary_columns(projected[1], places).astype(jnp.bfloat16)
    new_values = projected[2].astype(jnp.bfloat16)
    new_cache = jnp.stack(
        [new_keys.reshape(local, rows_here), new_values.reshape(local, rows_here)], axis=0
    )
    block_len = BS
    owned = pcache.shape[2] // block_len
    paged = pcache.reshape(2, local, owned, block_len)
    requests = block_table.shape[0]
    table_width = block_table.shape[1]
    slots_each = table_width // devices
    block_ids = here * owned + jnp.arange(owned, dtype=jnp.int32)
    matches = block_table[None, :, :] == block_ids[:, None, None]
    found = jnp.any(matches, axis=2)
    in_use = jnp.any(found, axis=1)
    owner = jnp.sum(jnp.where(found, jnp.arange(requests, dtype=jnp.int32)[None, :], 0), axis=1)
    logical = jnp.sum(
        jnp.where(matches, jnp.arange(table_width, dtype=jnp.int32)[None, None, :], 0), axis=(1, 2)
    )
    counter = jnp.arange(owned, dtype=jnp.int32)
    earlier = (
        (owner[:, None] == owner[None, :]) & in_use[None, :] & (counter[None, :] < counter[:, None])
    )
    standing = jnp.sum(earlier.astype(jnp.int32), axis=1)
    within_block = jnp.arange(block_len, dtype=jnp.int32)
    block_rows = min(rows_here, 512)
    count_blocks = rows_here // block_rows
    scale = HD ** (-0.5)
    query_blocks = jnp.transpose(
        queries.reshape(heads_here, HD, count_blocks, block_rows), (2, 0, 1, 3)
    )
    first_rows = jnp.arange(count_blocks, dtype=jnp.int32) * block_rows
    destination = owner * slots_each + standing
    routing = (destination[None, :] == jnp.arange(table_width, dtype=jnp.int32)[:, None]) & in_use[
        None, :
    ]
    outgoing = jnp.einsum(
        "wo,cfob->cfwb", routing.astype(jnp.bfloat16), paged, preferred_element_type=jnp.float32
    ).astype(jnp.bfloat16)
    outgoing = outgoing.reshape(2, local, table_width * block_len)
    labels = jnp.sum(jnp.where(routing, logical[None, :] + 1, 0), axis=1) - 1
    labels = labels.reshape(1, 1, table_width)
    blocks_in, labels_in = (
        lax.all_to_all(outgoing, "blk", split_axis=2, concat_axis=2, tiled=True),
        lax.all_to_all(labels, "blk", split_axis=2, concat_axis=2, tiled=True),
    )
    cached_keys = blocks_in[0].reshape(heads_here, HD, -1)
    cached_values = blocks_in[1].reshape(heads_here, HD, -1).astype(jnp.float32)
    label_flat = labels_in.reshape(-1)
    key_places = label_flat[:, None] * block_len + within_block[None, :]
    live = ((label_flat[:, None] >= 0) & (key_places < cache_len[0])).reshape(-1)
    old_mask = jnp.broadcast_to(live[None, :], (block_rows, live.shape[0]))
    new_values_f = new_values.astype(jnp.float32)

    def attend(inputs):
        query_block, first_row = inputs
        causal = (first_row + jnp.arange(block_rows, dtype=jnp.int32))[:, None] >= lines[None, :]
        old_part = softmax_part(query_block, cached_keys, cached_values, old_mask, scale)
        own_part = softmax_part(query_block, new_keys, new_values_f, causal, scale)
        return fold_softmax(old_part, own_part)

    mixed, highest, total = unblock(lax.map(attend, (query_blocks, first_rows)))
    attended = (mixed / total[:, None, :]).astype(jnp.bfloat16).reshape(local, rows_here)
    return (attended, new_cache)


def solution(mesh):
    in_specs = (
        P(None, "head", "blk"),
        P("head"),
        P(None, "head", None),
        P("blk"),
        P("head", "blk"),
        P(),
        P(None, "head", None),
        P(None, "head", "blk"),
        P(),
        P("blk"),
    )
    out_specs = (P("head", "blk"), P(None, "head", "blk"))
    return jax.shard_map(shards, mesh=mesh, in_specs=in_specs, out_specs=out_specs, check_vma=False)
```

profile of v0, /device:TPU:7, one launch (start us, length us, event | category | flops | bytes accessed | tf_op | source)
XLA Modules:
  0.0 287.5 jit_solution(1287686254156349032)
XLA Ops:
  7.2 0.0 copy-start
  7.2 0.0 reduce-scatter.4.cloned.1.call-start
  7.2 1.1 convert_reduce_fusion
  8.3 19.4 %all-reduce = (f32[4,128]{1,0:T(4,128)S(1)}, f32[4,128]{1,0:T(4,128)S(1)}) all-reduce(f32[4,128]{1,0:T(4,128)S(1)} %get-tuple-element.23, f32[4,128]{1,0:T(4,128)S(1)} %get-tuple-element.22), channel_id=1, replica_groups=mesh['head'=8,'blk'=64] {'head'}, use_global_device_ids=true, to_apply=%region_11.12 | all-reduce | flops 1024 | bytes 8192 | tf_op jit(solution)/shard_map/psum | solution.py:70
  27.8 1.5 convolution_bitcast_fusion
  29.3 1.1 copy.49
  30.5 0.0 reduce-scatter.4.cloned.1.call-update
  30.5 0.1 select_reduce_fusion.2
  30.6 0.7 copy.44
  31.3 14.9 %all-to-all-start.2 = ((s32[64,1,1]{2,1,0:T(1,128)}), s32[64,1,1]{2,1,0:T(1,128)S(1)}, u32[]{:S(2)}, u32[]{:S(2)}) async-start(s32[64,1,1]{2,1,0:T(1,128)} %copy.44), calls=%async_computation.2 | async-start | bytes 65536 | tf_op jit(solution)/shard_map/all_to_all | solution.py:107
  46.2 2.4 compare_reduce_fusion
  48.6 0.1 select_reduce_fusion.1
  48.7 0.2 convert_reduce_fusion.1
  48.9 1.4 fusion.8
  50.3 0.1 select_reduce_fusion
  50.4 0.7 copy.43
  51.2 3.7 %copy.38 = bf16[2,176,2048]{1,2,0:T(8,128)(2,1)} copy(bf16[2,176,2048]{2,1,0:T(8,128)(2,1)} %param.17) | data formatting | bytes 2883584 | tf_op args[7]
  54.9 13.5 %reduce-scatter.4.cloned.1.call-done = f32[176,128]{1,0:T(8,128)} async-done(((f32[1408,128]{1,0:T(8,128)}), f32[176,128]{1,0:T(8,128)}) %reduce-scatter.4.cloned.1.call-update) | async-done | bytes 90128
  68.4 1.0 copy.50
  69.4 0.1 reshape.265
  69.5 15.0 %all-to-all-start.1 = ((s32[1,1,128]{1,0,2:T(1,128)}), s32[1,1,128]{1,0,2:T(1,128)S(1)}, u32[]{:S(2)}, u32[]{:S(2)}) async-start(s32[1,1,128]{1,0,2:T(1,128)} %copy.43), calls=%async_computation.1 | async-start | bytes 131072 | tf_op jit(solution)/shard_map/all_to_all | solution.py:180
  84.5 0.3 convolution_convert_fusion.1
  84.8 0.8 reshape.266
  85.6 6.7 %all-to-all-done.1 = s32[1,1,128]{1,0,2:T(1,128)S(1)} async-done(((s32[1,1,128]{1,0,2:T(1,128)}), s32[1,1,128]{1,0,2:T(1,128)S(1)}, u32[]{:S(2)}, u32[]{:S(2)}) %all-to-all-start.1) | async-done | bytes 544 | tf_op jit(solution)/shard_map/all_to_all | solution.py:180
  92.2 6.6 %all-to-all-start.3 = ((bf16[64,4,176]{2,1,0:T(4,128)(2,1)}), bf16[64,4,176]{2,1,0:T(4,128)(2,1)S(1)}, u32[]{:S(2)}, u32[]{:S(2)}) async-start(bf16[64,4,176]{2,1,0:T(4,128)(2,1)} %reshape.266), calls=%async_computation.3 | async-start | bytes 262144 | tf_op jit(solution)/shard_map/all_to_all | solution.py:106
  98.8 4.9 %convert_bitcast_fusion = bf16[2,176,128,32]{2,1,3,0:T(8,128)(2,1)} fusion(bf16[2,176,64,32]{1,3,2,0:T(8,128)(2,1)} %bitcast.47, s32[64]{0:T(128)S(1)} %get-tuple-element.61, pred[64]{0:T(512)(128)(4,1)S(1)} %get-tuple-element.24), kind=kOutput, calls=%fused_computation.13 | convolution fusion | flops 186007552 | bytes 4325696 | tf_op jit(solution)/shard_map/wo,cfob->cfwb/dot_general | solution.py:172
  103.7 7.7 %copy.40 = bf16[2,176,128,32]{1,3,2,0:T(8,128)(2,1)} copy(bf16[2,176,128,32]{2,1,3,0:T(8,128)(2,1)} %convert_bitcast_fusion) | data formatting | bytes 5767168 | tf_op jit(solution)/shard_map/convert_element_type | solution.py:174
  111.4 10.1 %copy.41 = bf16[2,176,4096]{1,0,2:T(2,128)(2,1)} copy(bf16[2,176,4096]{1,2,0:T(8,128)(2,1)} %bitcast.46) | data formatting | bytes 5767168 | tf_op jit(solution)/shard_map/reshape | solution.py:175
  121.5 10.6 %all-to-all-start = ((bf16[2,176,4096]{1,0,2:T(2,128)(2,1)}), bf16[2,176,4096]{1,0,2:T(2,128)(2,1)}, u32[]{:S(2)}, u32[]{:S(2)}) async-start(bf16[2,176,4096]{1,0,2:T(2,128)(2,1)} %copy.41), calls=%async_computation | async-start | bytes 8388608 | tf_op jit(solution)/shard_map/all_to_all | solution.py:179
  132.2 0.0 all-gather.2.cloned.1.call-start
  132.2 0.8 dynamic_slice.9
  133.0 1.2 reduce.3
  134.2 0.1 broadcast_in_dim.182
  134.3 0.1 and.66
  134.4 0.1 iota_add_fusion
  134.5 0.1 add.170
  134.6 0.2 fusion.32
  134.8 0.1 reshape.267
  134.9 0.3 multiply_reduce_fusion
  135.2 13.1 %psum.23 = f32[512]{0:T(512)S(1)} all-reduce(f32[512]{0:T(512)S(1)} %get-tuple-element.55), channel_id=1, replica_groups=mesh['head'=8,'blk'=64] {'head'}, use_global_device_ids=true, to_apply=%region_14.15 | all-reduce | flops 512 | bytes 4096 | tf_op jit(solution)/shard_map/psum | solution.py:121
  148.4 0.8 multiply_convert_fusion
  149.2 0.0 all-gather.2.cloned.1.call-update
  149.9 0.1 iota_compare_fusion
  150.0 0.4 multiply_cosine_fusion
  150.4 2.4 multiply_reduce_fusion.1
  152.7 2.4 compare_reduce_fusion.2
  155.1 0.1 fusion.45
  155.2 0.1 and.63
  155.3 34.5 %all-gather.2.cloned.1.call-done = bf16[1408,512]{1,0:T(8,128)(2,1)} async-done(((bf16[176,512]{1,0:T(8,128)(2,1)}), bf16[1408,512]{1,0:T(8,128)(2,1)}) %all-gather.2.cloned.1.call-update) | async-done | bytes 1441808 | tf_op jit(solution)/shard_map/all_gather | solution.py:129
  189.8 2.8 fusion.15
  192.7 0.1 multiply_subtract_fusion
  192.9 0.8 pad_maximum_fusion
  193.6 0.1 subtract_convert_fusion
  193.7 0.6 fusion.10
  194.4 1.3 copy-done.1
  195.7 0.6 fusion.11
  196.3 31.6 %all-to-all-done = bf16[2,176,4096]{1,0,2:T(2,128)(2,1)} async-done(((bf16[2,176,4096]{1,0,2:T(2,128)(2,1)}), bf16[2,176,4096]{1,0,2:T(2,128)(2,1)}, u32[]{:S(2)}, u32[]{:S(2)}) %all-to-all-start) | async-done | bytes 2883616 | tf_op jit(solution)/shard_map/all_to_all | solution.py:179
  227.9 9.8 %fusion.66 = (bf16[1,176,4096]{1,0,2:T(2,128)(2,1)}, bf16[1,176,4096]{1,0,2:T(2,128)(2,1)}) fusion(bf16[2,176,4096]{1,0,2:T(2,128)(2,1)} %all-to-all-done), kind=kLoop, calls=%fused_computation.118 | loop fusion | bytes 5767168 | tf_op jit(solution)/shard_map/slice | solution.py:183
  237.7 9.6 %copy.42 = bf16[1,176,4096]{2,1,0:T(8,128)(2,1)} copy(bf16[1,176,4096]{1,0,2:T(2,128)(2,1)} %get-tuple-element.41) | data formatting | bytes 2883584 | tf_op jit(solution)/shard_map/slice | solution.py:183
  247.3 9.8 %copy.45 = bf16[1,176,4096]{2,1,0:T(8,128)(2,1)S(1)} copy(bf16[1,176,4096]{1,0,2:T(2,128)(2,1)} %get-tuple-element.42) | data formatting | bytes 2883584 | tf_op jit(solution)/shard_map/slice | solution.py:182
  257.1 3.7 %fusion = (f32[2,512]{1,0:T(2,128)S(1)}, f32[2,512,4096]{2,1,0:T(8,128)S(1)}) fusion(pred[4096]{0:T(1024)(128)(4,1)S(1)} %and.63, bf16[2,88,4096]{2,1,0:T(8,128)(2,1)S(1)} %bitcast.48, bf16[2,44,512]{2,1,0:T(8,128)(2,1)} %copy-done.8, bf16[2,44,512]{2,1,0:T(8,128)(2,1)S(1)} %get-tuple-element.45), kind=kOutput, calls=%fused_computation.2 | convolution fusion | flops 751139840 | bytes 18407424 | tf_op jit(solution)/shard_map/while/body/eval_jaxpr/hdq,hdk->hqk/dot_general | solution.py:32
  260.8 5.1 %fusion.1 = f32[2,512]{1,0:T(2,128)S(1)} fusion(f32[2,512,4096]{2,1,0:T(8,128)S(1)} %get-tuple-element.60, f32[2,512]{1,0:T(2,128)S(1)} %get-tuple-element.59, pred[4096]{0:T(1024)(128)(4,1)S(1)} %and.63), kind=kLoop, calls=%fused_computation.3 | loop fusion | flops 20970496 | bytes 16789504 | tf_op jit(solution)/shard_map/while/body/eval_jaxpr/reduce_sum | solution.py:37
  266.0 1.5 fusion.20
  267.5 13.2 %fusion.29 = bf16[2,88,512]{2,1,0:T(8,128)(2,1)} fusion(f32[2,88,512]{2,1,0:T(8,128)S(1)} %fusion.20, bf16[2,88,4096]{2,1,0:T(8,128)(2,1)S(1)} %bitcast.51, f32[2,512,4096]{2,1,0:T(8,128)S(1)} %get-tuple-element.60, f32[2,512]{1,0:T(2,128)S(1)} %get-tuple-element.59, pred[4096]{0:T(1024)(128)(4,1)S(1)} %and.63, f32[2,512]{1,0:T(2,128)S(1)} %get-tuple-element.28, ...), kind=kOutput, calls=%fused_computation.39 | convolution fusion | flops 4446322688 | bytes 18776064 | tf_op jit(solution)/shard_map/while/body/eval_jaxpr/hqk,hdk->hdq/dot_general | solution.py:38
  (38 shorter events, 0.3 us)
Async XLA Ops:
  7.2 20.6 %copy-start = (bf16[4,176,1408]{2,1,0:T(8,128)(2,1)S(1)}, bf16[4,176,1408]{2,1,0:T(8,128)(2,1)}, u32[]{:S(2)}) copy-start(bf16[4,176,1408]{2,1,0:T(8,128)(2,1)} %param.12) | copy-start | bytes 5947396
  7.2 61.2 %reduce-scatter.4.cloned.1.call-start = ((), (), s32[]{:S(2)}) async-start(), calls=%async_computation.6 | async-start | bytes 811008
  27.8 2.7 copy-start.11
  27.8 18.4 %copy-start.9 = (s32[64,128]{1,0:T(8,128)S(1)}, s32[64,128]{1,0:T(8,128)}, u32[]{:S(2)}) copy-start(s32[64,128]{1,0:T(8,128)} %param.18) | copy-start | bytes 98308
  31.3 38.2 %all-to-all-start.2 = ((s32[64,1,1]{2,1,0:T(1,128)}), s32[64,1,1]{2,1,0:T(1,128)S(1)}, u32[]{:S(2)}, u32[]{:S(2)}) async-start(s32[64,1,1]{2,1,0:T(1,128)} %copy.44), calls=%async_computation.2 | async-start | bytes 65536 | tf_op jit(solution)/shard_map/all_to_all | solution.py:107
  69.5 22.7 %all-to-all-start.1 = ((s32[1,1,128]{1,0,2:T(1,128)}), s32[1,1,128]{1,0,2:T(1,128)S(1)}, u32[]{:S(2)}, u32[]{:S(2)}) async-start(s32[1,1,128]{1,0,2:T(1,128)} %copy.43), calls=%async_computation.1 | async-start | bytes 131072 | tf_op jit(solution)/shard_map/all_to_all | solution.py:180
  92.2 29.3 %all-to-all-start.3 = ((bf16[64,4,176]{2,1,0:T(4,128)(2,1)}), bf16[64,4,176]{2,1,0:T(4,128)(2,1)S(1)}, u32[]{:S(2)}, u32[]{:S(2)}) async-start(bf16[64,4,176]{2,1,0:T(4,128)(2,1)} %reshape.266), calls=%async_computation.3 | async-start | bytes 262144 | tf_op jit(solution)/shard_map/all_to_all | solution.py:106
  121.5 13.4 %copy-start.10 = (bf16[176,512]{1,0:T(8,128)(2,1)S(1)}, bf16[176,512]{1,0:T(8,128)(2,1)}, u32[]{:S(2)}) copy-start(bf16[176,512]{1,0:T(8,128)(2,1)} %param.14) | copy-start | bytes 540676
  121.5 106.4 %all-to-all-start = ((bf16[2,176,4096]{1,0,2:T(2,128)(2,1)}), bf16[2,176,4096]{1,0,2:T(2,128)(2,1)}, u32[]{:S(2)}, u32[]{:S(2)}) async-start(bf16[2,176,4096]{1,0,2:T(2,128)(2,1)} %copy.41), calls=%async_computation | async-start | bytes 8388608 | tf_op jit(solution)/shard_map/all_to_all | solution.py:179
  132.2 57.6 %all-gather.2.cloned.1.call-start = ((), (), s32[]{:S(2)}) async-start(), calls=%async_computation.5 | async-start | bytes 1622016 | tf_op jit(solution)/shard_map/all_gather | solution.py:129
  150.0 44.4 %copy-start.4 = (pred[512,512]{0,1:T(8,128)(4,1)}, pred[512,512]{0,1:T(8,128)(4,1)S(1)}, u32[]{:S(2)}) copy-start(pred[512,512]{0,1:T(8,128)(4,1)S(1)} %iota_compare_fusion) | copy-start | bytes 786436
  192.7 1.0 copy-start.6
  193.7 2.6 copy-start.8
  194.4 1.4 copy-start.1
  260.8 5.2 %copy-start.2 = (f32[2,512,512]{1,2,0:T(8,128)S(1)}, f32[2,512,512]{1,2,0:T(8,128)}, u32[]{:S(2)}) copy-start(f32[2,512,512]{1,2,0:T(8,128)} %copy-done.1) | copy-start | bytes 6291460
  260.8 5.2 %copy-start.5 = (pred[512,512]{0,1:T(8,128)(4,1)S(1)}, pred[512,512]{0,1:T(8,128)(4,1)}, u32[]{:S(2)}) copy-start(pred[512,512]{0,1:T(8,128)(4,1)} %copy-done.4) | copy-start | bytes 786436
  260.8 5.2 %copy-start.7 = (bf16[1,176,512]{2,1,0:T(8,128)(2,1)S(1)}, bf16[1,176,512]{2,1,0:T(8,128)(2,1)}, u32[]{:S(2)}) copy-start(bf16[1,176,512]{2,1,0:T(8,128)(2,1)} %copy-done.6) | copy-start | bytes 540676
  266.0 1.5 copy-start.3
Sparse Core Ops, SparseCore 0:
  30.6 37.6 reduce-scatter.3
  149.3 40.4 all-gather.1
where the time goes:
time: 290 us; the launch traced here: 288 us
  waiting for transfers between devices  86.3 us (30%)
  local copies, waits for them, and re-layouts  57.9 us (20%)
  starting transfers between devices  47.2 us (16%)
  blocking collectives  32.6 us (11%)
  matrix products  28.9 us (10%)
  other arithmetic  19.6 us (7%)
  between operations  15.1 us (5%)
    all_gather x1, waiting for transfers between devices, shards(): lax.all_gather(normed, 'head', axis=0, tiled=True)  34.5 us
    all_to_all x1, waiting for transfers between devices, shards(): lax.all_to_all(outgoing, 'blk', split_axis=2, concat_axis=2, tiled=True)  31.6 us
    psum x1, blocking collectives, shards(): lax.psum((jnp.sum(floats, axis=1), jnp.sum(floats * floats, axis=1)), 'he...  19.4 us
    slice x2, local copies, waits for them, and re-layouts, shards(): cached_values = blocks_in[1].reshape(heads_here, HD, -1).astype(jnp.float32)  19.4 us
    all_to_all x1, starting transfers between devices, shards(): lax.all_to_all(labels, 'blk', split_axis=2, concat_axis=2, tiled=True)  15 us
    all_to_all x1, starting transfers between devices, shards(): lax.all_to_all(starts, 'blk', split_axis=0, concat_axis=0, tiled=True)  14.9 us
    dot_general x2, matrix products, softmax_part(): jnp.einsum('hqk,hdk->hdq', expo, values, precision=lax.Precision.HIGHEST)  14.7 us
    unnamed x3, waiting for transfers between devices  13.5 us
  transfers between devices with their start and end apart: 6, of which 4 were waited for; matrix products, arithmetic and copies ran while one was open for 17% of the time, Pallas kernels for 0%

commit v1 on v0

v1 whole, which is shorter than its diff:
```python
import functools
import math

import jax
import jax.numpy as jnp
from jax import lax
from jax.experimental import pallas as pl
from jax.experimental.pallas import tpu as pltpu
from jax.sharding import PartitionSpec as P

HD = 88
BS = 32
MESH = pl.DeviceIdType.MESH
GRID = {64: (4, 8, 2), 8: (2, 2, 2)}
F32 = jnp.float32
BF16 = jnp.bfloat16
NEG = -1e30


def dot(a, b, ca=1, cb=0):
    return lax.dot_general(a, b, (((ca,), (cb,)), ((), ())), preferred_element_type=F32)


def iota(shape, dim):
    return lax.broadcasted_iota(jnp.int32, shape, dim)


def comm_kernel(
    width,
    rows_here,
    idx_ref,
    image_slot_ref,
    gain_ref,
    vision_hbm,
    proj_hbm,
    pcache_hbm,
    slots_out,
    extra_out,
    img_out,
    meta_out,
    vision,
    proj,
    pcache,
    staged,
    outgoing,
    stats,
    stats_in,
    parts,
    parts_in,
    pieces,
    pieces_in,
    img,
    load_sem,
    local_sem,
    send_sem,
    recv_sem,
):
    z = lax.axis_index("head")
    me = lax.axis_index("blk")
    zs = stats_in.shape[0]
    devices = slots_out.shape[0]
    cs, xs, ys = extra_out.shape[:3]
    my_c = lax.rem(me, cs)
    my_y = lax.rem(me // cs, ys)
    my_x = me // (cs * ys)
    local = vision.shape[1]
    groups = vision.shape[2]

    load_vision = pltpu.make_async_copy(vision_hbm, vision, load_sem.at[0])
    load_pcache = pltpu.make_async_copy(pcache_hbm, pcache, load_sem.at[1])
    load_proj = pltpu.make_async_copy(proj_hbm, proj, load_sem.at[2])
    load_vision.start()
    load_pcache.start()
    load_proj.start()

    barrier = pltpu.get_barrier_semaphore()

    @pl.loop(1, devices)
    def _(step):
        pl.semaphore_signal(
            barrier, inc=1, device_id=(z, lax.rem(me + step, devices)), device_id_type=MESH
        )

    @pl.loop(1, zs)
    def _(step):
        pl.semaphore_signal(
            barrier, inc=1, device_id=(lax.rem(z + step, zs), me), device_id_type=MESH
        )

    def send(src, dst, phase, device):
        return pltpu.make_async_remote_copy(
            src_ref=src,
            dst_ref=dst,
            send_sem=send_sem.at[phase],
            recv_sem=recv_sem.at[phase],
            device_id=device,
            device_id_type=MESH,
        )

    def over_z(src_of, dst, phase):
        @pl.loop(1, zs)
        def _(step):
            other = lax.rem(z + step, zs)
            send(src_of(other), dst, phase, (other, me)).start()

    def await_in(ref, phase):
        send(ref, ref, phase, (z, me)).wait_recv()

    def await_out(ref, phase):
        send(ref, ref, phase, (z, me)).wait_send()

    load_vision.wait()
    sums, squares = [], []
    for t in range(4):
        rows = vision[t].astype(F32)
        sums.append(jnp.sum(rows, axis=0, keepdims=True))
        squares.append(jnp.sum(rows * rows, axis=0, keepdims=True))
    stats[...] = jnp.concatenate(sums + squares, axis=0)
    stats_in[pl.ds(z, 1)] = stats[...][None]
    pl.semaphore_wait(barrier, devices - 1 + zs - 1)
    over_z(lambda other: stats, stats_in.at[z], 0)

    load_pcache.wait()

    @pl.loop(0, pcache.shape[2] // 128)
    def _(column):
        lanes = pl.ds(pl.multiple_of(column * 128, 128), 128)
        tiles = [pcache[j, :, lanes] for j in range(4)]
        for o in range(4):
            staged[column * 4 + o] = jnp.concatenate(
                [tile[:, o * BS : (o + 1) * BS] for tile in tiles], axis=1
            )

    outgoing[devices] = staged[idx_ref[devices]]
    own_extra = pltpu.make_async_copy(
        outgoing.at[devices], extra_out.at[my_c, my_x, my_y], local_sem.at[0]
    )
    own_extra.start()

    @pl.loop(1, ys)
    def _(step):
        other = (my_x * ys + lax.rem(my_y + step, ys)) * cs + my_c
        send(outgoing.at[devices], extra_out.at[my_c, my_x, my_y], 4, (z, other)).start()

    @pl.loop(1, devices)
    def _(step):
        other = lax.rem(me + step, devices)
        outgoing[other] = staged[idx_ref[other]]
        send(outgoing.at[other], slots_out.at[me], 1, (z, other)).start()

    outgoing[me] = staged[idx_ref[me]]
    own_slot = pltpu.make_async_copy(outgoing.at[me], slots_out.at[me], local_sem.at[1])
    own_slot.start()

    square = iota((local, local), 0) == iota((local, local), 1)
    gain = jnp.sum(jnp.where(square, gain_ref[...], 0.0), axis=1, keepdims=True)
    load_proj.wait()
    await_in(stats_in.at[pl.ds(0, zs - 1)], 0)
    total = jnp.sum(stats_in[...], axis=0) / width
    average = total[0:4]
    scale = lax.rsqrt(total[4:8] - average * average + 1e-06)
    normed = jnp.concatenate(
        [
            (vision[t].astype(F32) - average[t : t + 1]) * scale[t : t + 1] * gain
            for t in range(4)
        ],
        axis=0,
    ).astype(BF16)
    partial_rows = dot(normed, proj[...], 0, 0)
    partial_columns = jnp.transpose(partial_rows)
    parts[...] = partial_columns.astype(BF16).reshape(parts.shape)
    parts_in[pl.ds(z, 1)] = parts[pl.ds(z, 1)]
    over_z(lambda other: parts.at[other], parts_in.at[z], 2)

    own_extra.wait()
    await_in(extra_out.at[0, 0, pl.ds(0, ys - 1)], 4)

    @pl.loop(1, xs)
    def _(step):
        other = (lax.rem(my_x + step, xs) * ys + my_y) * cs + my_c
        send(extra_out.at[my_c, my_x], extra_out.at[my_c, my_x], 5, (z, other)).start()

    count = image_slot_ref.shape[1]
    spread = (iota((count, groups), 1) // 4 == iota((count, groups), 0)).astype(BF16)
    slot = image_slot_ref[...]
    target = dot((slot // rows_here).astype(F32).astype(BF16), spread)
    place = dot((lax.rem(slot, rows_here) // 4 + 1).astype(F32).astype(BF16), spread)
    diagonal = iota((groups, groups), 0) == iota((groups, groups), 1)
    place_column = jnp.sum(jnp.where(diagonal, place, 0.0), axis=1, keepdims=True)
    line = iota((devices * 8, 2 * groups), 0)
    column = iota((devices * 8, 2 * groups), 1)
    wanted = jnp.concatenate([target, target], axis=1).astype(jnp.int32)
    half = (column >= groups).astype(jnp.int32) * 4
    select = ((line // 8) == wanted) & (lax.rem(line, 8) == (lax.rem(column, 4) + half))
    await_in(parts_in.at[pl.ds(0, zs - 1)], 2)
    merged = jnp.sum(parts_in[...].astype(F32), axis=0)
    high = jnp.concatenate(
        [merged[128:], jnp.zeros((256 - local, groups), F32)], axis=0
    )
    merged_rows = jnp.transpose(merged[:128])
    high_rows = jnp.transpose(high)
    high_rows = jnp.where(iota((groups, 128), 1) == local - 128, place_column, high_rows)
    both = jnp.concatenate([merged_rows, high_rows], axis=0).astype(BF16)
    pieces[...] = dot(select.astype(F32).astype(BF16), both).astype(BF16).reshape(pieces.shape)
    pieces_in[pl.ds(me, 1)] = pieces[pl.ds(me, 1)]

    @pl.loop(1, devices)
    def _(step):
        other = lax.rem(me + step, devices)
        send(pieces.at[other], pieces_in.at[me], 3, (z, other)).start()

    await_in(extra_out.at[0, pl.ds(0, xs - 1)], 5)
    last = send(
        extra_out.at[my_c], extra_out.at[my_c], 6, (z, (my_x * ys + my_y) * cs + (cs - 1 - my_c))
    )
    last.start()

    span = devices * 8
    earlier = (iota((span, span), 0) // 8 < iota((span, span), 1) // 8) & (
        lax.rem(iota((span, span), 0), 8) == 4
    )
    same = (iota((span, span), 0) // 8 == iota((span, span), 1) // 8) & (
        lax.rem(iota((span, span), 0), 8) == 4
    )
    earlier = earlier.astype(F32).astype(BF16)
    same = same.astype(F32).astype(BF16)
    await_in(pieces_in.at[pl.ds(0, devices - 1)], 3)
    arrived = jnp.transpose(pieces_in[...].reshape(span, 128).astype(F32)).astype(BF16)
    marks = jnp.broadcast_to(arrived[local - 128 : local - 127].astype(F32), (8, span))
    present = (marks > 0.0).astype(F32)
    rank = dot(present.astype(BF16), earlier)[0:1]
    mark = dot(marks.astype(BF16), same)
    within = lax.rem(iota((groups, span), 1), 8)
    order = jnp.where(mark[0:1] > 0.0, rank, -1.0).astype(jnp.int32) * 4
    first = (within < 4) & (iota((groups, span), 0) == order + within)
    second = (within >= 4) & (iota((groups, span), 0) == order + within - 4)
    first = first.astype(F32).astype(BF16)
    second = second.astype(F32).astype(BF16)
    low = dot(arrived, first, 1, 1)
    high = dot(arrived, second, 1, 1)
    img[...] = jnp.concatenate([low, high[: local - 128]], axis=0).astype(BF16)
    meta_out[...] = dot(mark.astype(BF16), first, 1, 1)
    own_img = pltpu.make_async_copy(img, img_out.at[z], local_sem.at[2])
    own_img.start()
    over_z(lambda other: img, img_out.at[z], 7)

    await_in(img_out.at[pl.ds(0, zs - 1)], 7)
    await_in(slots_out.at[pl.ds(0, devices - 1)], 1)
    last.wait_recv()
    own_slot.wait()
    own_img.wait()
    await_out(stats_in.at[pl.ds(0, zs - 1)], 0)
    await_out(slots_out.at[pl.ds(0, devices - 1)], 1)
    await_out(parts_in.at[pl.ds(0, zs - 1)], 2)
    await_out(pieces_in.at[pl.ds(0, devices - 1)], 3)
    await_out(extra_out.at[0, 0, pl.ds(0, ys - 1)], 4)
    await_out(extra_out.at[0, pl.ds(0, xs - 1)], 5)
    last.wait_send()
    await_out(img_out.at[pl.ds(0, zs - 1)], 7)


def communicate(width, rows, indices, image_slot, ln_gain, vision, merge_proj, pcache, devices, zs):
    xs, ys, cs = GRID[devices]
    _, local, groups = vision.shape
    vmem = pltpu.VMEM
    anywhere = pl.BlockSpec(memory_space=pl.ANY)
    inside = pl.BlockSpec(memory_space=pltpu.VMEM)
    tile = (HD, 4 * BS)
    blocks = pcache.shape[2] // BS
    return pl.pallas_call(
        functools.partial(comm_kernel, width, rows),
        out_shape=(
            jax.ShapeDtypeStruct((devices,) + tile, BF16),
            jax.ShapeDtypeStruct((cs, xs, ys) + tile, BF16),
            jax.ShapeDtypeStruct((zs, local, groups), BF16),
            jax.ShapeDtypeStruct((8, groups), F32),
        ),
        in_specs=[pl.BlockSpec(memory_space=pltpu.SMEM), inside, inside, anywhere, anywhere, anywhere],
        out_specs=(anywhere, anywhere, anywhere, inside),
        scratch_shapes=[
            vmem(vision.shape, BF16),
            vmem(merge_proj.shape, BF16),
            vmem(pcache.shape, BF16),
            vmem((blocks,) + tile, BF16),
            vmem((devices + 1,) + tile, BF16),
            vmem((8, groups), F32),
            vmem((zs, 8, groups), F32),
            vmem((zs, local, groups), BF16),
            vmem((zs, local, groups), BF16),
            vmem((devices, 8, 128), BF16),
            vmem((devices, 8, 128), BF16),
            vmem((local, groups), BF16),
            pltpu.SemaphoreType.DMA((3,)),
            pltpu.SemaphoreType.DMA((3,)),
            pltpu.SemaphoreType.DMA((8,)),
            pltpu.SemaphoreType.DMA((8,)),
        ],
        compiler_params=pltpu.CompilerParams(
            collective_id=0, has_side_effects=True, vmem_limit_bytes=48 << 20
        ),
        name="exchange",
    )(indices, image_slot, ln_gain, vision, merge_proj, pcache)


def attend_kernel(
    grid,
    counts_ref,
    text_ref,
    img_ref,
    meta_ref,
    gain_ref,
    weight_ref,
    cosine_ref,
    sine_ref,
    slots_ref,
    extra_hbm,
    attended_ref,
    cache_ref,
    extra,
    keys,
    values,
    scores,
    normed_ref,
    extra_sem,
):
    xs, ys, cs = grid
    devices = slots_ref.shape[0]
    width, rows = text_ref.shape
    groups = img_ref.shape[1]
    old = devices * BS
    heads = keys.shape[0]
    longest = counts_ref[2 * devices] > 0
    load_extra = pltpu.make_async_copy(extra_hbm, extra, extra_sem)

    @pl.when(longest)
    def _():
        load_extra.start()

    diagonal = iota((groups, groups), 0) == iota((groups, groups), 1)
    mark = jnp.sum(jnp.where(diagonal, meta_ref[0:1], 0.0), axis=1, keepdims=True)
    row_of = (mark.astype(jnp.int32) - 1) * 4 + lax.rem(iota((groups, 1), 0), 4)
    hits = (iota((groups, rows), 1) == row_of).astype(F32)
    covered = jnp.sum(hits, axis=0, keepdims=True) > 0.0
    hits = hits.astype(BF16)
    squares = jnp.zeros((8, rows), F32)
    step = width // gain_ref.shape[0]
    for s in range(width // step):
        lines = slice(s * step, (s + 1) * step)
        placed = jnp.where(covered, dot(img_ref[lines], hits), text_ref[lines].astype(F32))
        squares = squares + jnp.sum((placed * placed).reshape(step // 8, 8, rows), axis=0)
        normed_ref[lines] = placed.astype(BF16)
    mean_square = jnp.sum(squares, axis=0, keepdims=True) / width
    scale = lax.rsqrt(mean_square + 1e-06)
    gains = jnp.transpose(gain_ref[...])
    for s in range(width // step):
        lines = slice(s * step, (s + 1) * step)
        normed_ref[lines] = (
            normed_ref[lines].astype(F32) * scale * gains[:, s : s + 1]
        ).astype(BF16)

    projected = dot(weight_ref[...], normed_ref[...])
    local = heads * HD
    cosine = cosine_ref[...]
    sine = sine_ref[...]

    def rotate(x):
        a = x[: HD // 2]
        b = x[HD // 2 :]
        return jnp.concatenate([a * cosine - b * sine, b * cosine + a * sine], axis=0)

    bias_lane = (iota((rows, 128 - HD), 1) == 0).astype(F32)
    queries = []
    for h in range(heads):
        query = rotate(projected[h * HD : (h + 1) * HD]).astype(BF16).astype(F32)
        query = jnp.transpose(query)
        queries.append(jnp.concatenate([query, bias_lane], axis=1).astype(BF16))
        key = rotate(projected[local + h * HD : local + (h + 1) * HD]).astype(BF16)
        value = projected[2 * local + h * HD : 2 * local + (h + 1) * HD].astype(BF16)
        cache_ref[0, h * HD : (h + 1) * HD] = key
        cache_ref[1, h * HD : (h + 1) * HD] = value
        keys[h, 0:HD, 0:rows] = key
        keys[h, HD:, 0:rows] = jnp.zeros((128 - HD, rows), BF16)
        values[h, :, 0:rows] = value

    lane = iota((128 - HD, 128), 1)
    top = iota((128 - HD, 128), 0) == 0

    def unpack(tile_of, count_of, column):
        tiles = [tile_of(w) for w in range(4)]
        limit = count_of(3)
        for w in (2, 1, 0):
            limit = jnp.where(lane < (w + 1) * BS, count_of(w), limit)
        bias = jnp.where(top & (lax.rem(lane, BS) >= limit), NEG, 0.0).astype(BF16)
        lanes = pl.ds(pl.multiple_of(column * 128, 128), 128)
        for h in range(heads):
            keys[h, 0:HD, lanes] = jnp.concatenate(
                [tile[:, h * BS : (h + 1) * BS] for tile in tiles], axis=1
            )
            keys[h, HD:, lanes] = bias
            at = (heads + h) * BS
            values[h, :, lanes] = jnp.concatenate(
                [tile[:, at : at + BS] for tile in tiles], axis=1
            )

    @pl.loop(0, devices // 4)
    def _(g):
        unpack(
            lambda w: slots_ref[g * 4 + w], lambda w: counts_ref[g * 4 + w], rows // 128 + g
        )

    @pl.when(longest)
    def _():
        load_extra.wait()

        @pl.loop(0, devices // 4)
        def _(g):
            def source(w):
                e = g * 4 + w
                c = e // (xs * ys)
                return lax.rem(e, xs * ys) * cs + c

            unpack(
                lambda w: extra[g * 4 + w],
                lambda w: counts_ref[devices + source(w)],
                rows // 128 + devices // 4 + g,
            )

    factor = HD ** (-0.5) * math.log2(math.e)
    half = min(256, rows)
    chunk = min(512, old)
    chunks = old // chunk + jnp.where(longest, old // chunk, 0)
    causal = iota((half, rows), 0) - iota((half, rows), 1)

    def fold(x, op):
        out = x[:, 0:128]
        for s in range(1, x.shape[1] // 128):
            out = op(out, x[:, s * 128 : (s + 1) * 128])
        return out

    for part in range(rows // half):
        q = [query[part * half : (part + 1) * half] for query in queries]
        tops = []
        for h in range(heads):
            own = dot(q[h], keys[h, :, 0:rows])
            own = jnp.where(causal >= -part * half, own, NEG)
            scores[h, :, 0:rows] = own
            tops.append(fold(own, jnp.maximum))

        def first_pass(n, tops):
            lanes = pl.ds(pl.multiple_of(rows + n * chunk, 128), chunk)
            out = []
            for h in range(heads):
                s = dot(q[h], keys[h, :, lanes])
                scores[h, :, lanes] = s
                out.append(jnp.maximum(tops[h], fold(s, jnp.maximum)))
            return out

        tops = lax.fori_loop(0, chunks, first_pass, tops)
        tops = [jnp.max(t, axis=1, keepdims=True) * factor for t in tops]

        def weigh(h, lanes):
            p = jnp.exp2(scores[h, :, lanes] * factor - tops[h])
            return dot(p.astype(BF16), values[h, :, lanes], 1, 1), fold(p, jnp.add)

        carry = []
        for h in range(heads):
            carry += list(weigh(h, slice(0, rows)))

        def second_pass(n, carry):
            lanes = pl.ds(pl.multiple_of(rows + n * chunk, 128), chunk)
            out = []
            for h in range(heads):
                mixed, total = weigh(h, lanes)
                out += [carry[2 * h] + mixed, carry[2 * h + 1] + total]
            return out

        carry = lax.fori_loop(0, chunks, second_pass, carry)
        for h in range(heads):
            mixed = carry[2 * h] / jnp.sum(carry[2 * h + 1], axis=1, keepdims=True)
            attended_ref[h * HD : (h + 1) * HD, part * half : (part + 1) * half] = jnp.transpose(
                mixed
            ).astype(BF16)


def attend(counts, text, img, meta, gain, weights, cosine, sine, slots, extra, grid):
    width, rows = text.shape
    local = weights.shape[0] // 3
    heads = local // HD
    devices = slots.shape[0]
    total = rows + 2 * devices * BS
    inside = pl.BlockSpec(memory_space=pltpu.VMEM)
    return pl.pallas_call(
        functools.partial(attend_kernel, grid),
        out_shape=(
            jax.ShapeDtypeStruct((local, rows), BF16),
            jax.ShapeDtypeStruct((2, local, rows), BF16),
        ),
        in_specs=[pl.BlockSpec(memory_space=pltpu.SMEM)]
        + [inside] * 8
        + [pl.BlockSpec(memory_space=pl.ANY)],
        out_specs=(inside, inside),
        scratch_shapes=[
            pltpu.VMEM(extra.shape, BF16),
            pltpu.VMEM((heads, 128, total), BF16),
            pltpu.VMEM((heads, HD, total), BF16),
            pltpu.VMEM((heads, min(256, rows), total), F32),
            pltpu.VMEM((width, rows), BF16),
            pltpu.SemaphoreType.DMA,
        ],
        compiler_params=pltpu.CompilerParams(vmem_limit_bytes=56 << 20),
        name="attend",
    )(counts, text, img, meta, gain, weights, cosine, sine, slots, extra)


def shards(
    vision, ln_gain, merge_proj, image_slot, text, rms_gain, wqkv, pcache, block_table, cache_len
):
    zs = lax.axis_size("head")
    devices = lax.axis_size("blk")
    here = lax.axis_index("blk")
    local, rows = text.shape
    width = local * zs
    owned = pcache.shape[2] // BS
    full_text = lax.all_gather(text, "head", axis=0, tiled=True)

    columns = block_table.shape[1]
    column = jnp.arange(columns, dtype=jnp.int32)[None, :]
    mine = (block_table >= 0) & (block_table // owned == here)
    key = column * owned + block_table % owned
    none = columns * owned
    first = jnp.min(jnp.where(mine, key, none), axis=1)
    twice = jnp.sum(mine.astype(jnp.int32), axis=1) > 1
    second = jnp.max(jnp.where(mine & twice[:, None], key, -1))
    indices = jnp.concatenate(
        [
            jnp.where(first < none, first % owned, 0),
            jnp.where(second >= 0, second % owned, 0)[None],
        ]
    )

    table_row = lax.dynamic_index_in_dim(block_table, here, 0, keepdims=True)
    held = (table_row >= 0) & (
        table_row // owned == jnp.arange(devices, dtype=jnp.int32)[:, None]
    )
    low = jnp.min(jnp.where(held, column, columns), axis=1)
    high = jnp.max(jnp.where(held, column, -1), axis=1)
    length = cache_len[0]
    valid = jnp.clip(length - low * BS, 0, BS)
    valid_second = jnp.where(high > low, jnp.clip(length - high * BS, 0, BS), 0)
    counts = jnp.concatenate([valid, valid_second, jnp.max(valid_second)[None]])

    half = HD // 2
    inverse = jnp.exp(jnp.arange(half, dtype=F32) * (-2.0 * math.log(10000.0) / HD))
    places = (length + jnp.arange(rows, dtype=jnp.int32)).astype(F32)
    angles = inverse[:, None] * places[None, :]
    cosine, sine = jnp.cos(angles), jnp.sin(angles)

    slots, extra, img, meta = communicate(
        width,
        rows,
        indices,
        image_slot.reshape(1, -1),
        ln_gain.reshape(1, local),
        vision,
        merge_proj.reshape(4 * local, width),
        pcache.reshape(4, HD, -1),
        devices,
        zs,
    )
    return attend(
        counts,
        full_text,
        img.reshape(width, -1),
        meta,
        rms_gain.reshape(zs, local),
        wqkv.reshape(3 * local, width),
        cosine,
        sine,
        slots,
        extra.reshape(slots.shape),
        GRID[devices],
    )


def solution(mesh):
    in_specs = (
        P(None, "head", "blk"),
        P("head"),
        P(None, "head", None),
        P("blk"),
        P("head", "blk"),
        P(),
        P(None, "head", None),
        P(None, "head", "blk"),
        P(),
        P("blk"),
    )
    out_specs = (P("head", "blk"), P(None, "head", "blk"))
    return jax.shard_map(shards, mesh=mesh, in_specs=in_specs, out_specs=out_specs, check_vma=False)
```

time: 290 us -> 126 us (0.43)
  the two profiles are of different devices: /device:TPU:7 before, /device:TPU:3 now
where the time goes in v1:
time: 126 us; the launch traced here: 125 us
  Pallas kernels  91.6 us (73%)
  between operations  17.3 us (14%)
  local copies, waits for them, and re-layouts  8.5 us (7%)
  other arithmetic  7.04 us (6%)
    pallas_call x1, Pallas kernels, communicate(): pl.pallas_call(functools.partial(comm_kernel, width, rows), out_shape=(ja...  69.1 us
    pallas_call x1, Pallas kernels, attend(): pl.pallas_call(functools.partial(attend_kernel, grid), out_shape=(jax.Sha...  22.5 us
    unnamed x16, local copies, waits for them, and re-layouts  7.13 us
  transfers between devices with their start and end apart: 1, of which 0 were waited for; matrix products, arithmetic and copies ran while one was open for 7% of the time, Pallas kernels for 55%

profile of v1, /device:TPU:3, one launch (start us, length us, event | category | flops | bytes accessed | tf_op | source)
XLA Modules:
  0.0 125.2 jit_solution(2705853987679927163)
XLA Ops:
  7.2 0.0 all-gather.2.cloned.1.call-start
  7.2 0.7 all-gather.2.cloned.1.call-update
  7.9 0.9 convert_reduce_fusion
  8.8 1.5 %select_reduce_fusion.1 = (s32[64]{0:T(128)S(1)}, s32[]{:T(128)}) fusion(pred[64,128]{1,0:T(8,128)(4,1)S(1)} %get-tuple-element.15, s32[64,128]{1,0:T(8,128)} %param.18, s32[128]{0:T(128)S(1)} %iota_multiply_fusion, pred[64]{0:T(512)(128)(4,1)S(1)} %broadcast_compare_fusion), kind=kLoop, calls=%fused_computation.11 | loop fusion | flops 139199 | bytes 41796 | tf_op jit(solution)/shard_map/reduce_min | solution.py:531
  13.5 1.4 %reshape.51.gain_ref = f32[8,176]{1,0:T(8,128)} reshape(f32[1408]{0:T(1024)} %param.15) | data formatting | bytes 11264 | tf_op jit(solution)/shard_map/reshape | solution.py:575
  14.9 0.1 pad_add_fusion.1.idx_ref
  15.0 0.0 copy-start
  15.0 1.4 %copy-done = bf16[2,176,2048]{2,1,0:T(8,128)(2,1)S(1)} copy-done((bf16[2,176,2048]{2,1,0:T(8,128)(2,1)S(1)}, bf16[2,176,2048]{2,1,0:T(8,128)(2,1)}, u32[]{:S(2)}) %copy-start) | copy-done | bytes 1441816
  16.4 0.0 copy-start.4
  16.4 0.9 copy-done.4
  17.3 0.0 copy-start.6
  17.3 0.7 copy-done.6
  18.0 0.0 copy-start.7
  18.0 0.7 copy-done.7
  18.6 69.1 %exchange.1 = (bf16[64,88,128]{2,1,0:T(8,128)(2,1)S(1)}, bf16[2,4,8,88,128]{4,3,2,1,0:T(8,128)(2,1)S(1)}, bf16[8,176,128]{2,1,0:T(8,128)(2,1)S(1)}, f32[8,128]{1,0:T(8,128)S(1)}) custom-call(s32[65]{0:T(128)S(1)} %pad_add_fusion.1.idx_ref, s32[1,32]{1,0:T(1,128)S(1)} %bitcast.20, f32[1,176]{1,0:T(1,128)S(1)} %bitcast.19, bf16[4,176,128]{2,1,0:T(8,128)(2,1)S(1)} %copy-done.4, ...), custom_call_target="tpu_custom_call" | custom-call | tf_op jit(solution)/shard_map/exchange/pallas_call | solution.py:270
  87.7 0.0 copy-start.1
  87.7 1.1 copy-done.1
  88.8 0.0 copy-start.2
  88.8 1.1 copy-done.2
  89.9 0.0 copy-start.3
  89.9 0.7 copy-done.3
  90.6 0.0 copy-start.5
  90.6 0.6 copy-done.5
  91.2 0.7 fusion.6
  91.9 0.7 compare_bitcast_fusion
  92.6 0.1 select_reduce_fusion.3
  92.8 0.6 fusion.7
  93.4 1.3 %pad_add_fusion.counts_ref = s32[129]{0:T(256)} fusion(s32[1]{0:T(128)} %bitcast.3, s32[64]{0:T(128)S(1)} %get-tuple-element.17, s32[64]{0:T(128)S(1)} %get-tuple-element.20), kind=kLoop, calls=%fused_computation.31 | loop fusion | flops 258 | bytes 1032 | tf_op jit(solution)/shard_map/concatenate | solution.py:550
  94.7 1.1 multiply_sine_fusion
  95.8 0.0 all-gather.2.cloned.1.call-done.text_ref
  95.8 22.5 %attend.1 = (bf16[176,512]{1,0:T(8,128)(2,1)}, bf16[2,176,512]{2,1,0:T(8,128)(2,1)}) custom-call(s32[129]{0:T(256)} %pad_add_fusion.counts_ref, bf16[1408,512]{1,0:T(8,128)(2,1)} %all-gather.2.cloned.1.call-done.text_ref, bf16[1408,128]{1,0:T(8,128)(2,1)} %bitcast.18, f32[8,128]{1,0:T(8,128)} %copy-done.5, f32[8,176]{1,0:T(8,128)} %reshape.51.gain_ref, ...), custom_call_target="tpu_custom_call" | custom-call | tf_op jit(solution)/shard_map/attend/pallas_call | solution.py:492
  (5 shorter events, 0.0 us)
Async XLA Ops:
  7.2 88.7 %all-gather.2.cloned.1.call-start = ((), (), s32[]{:S(2)}) async-start(), calls=%async_computation | async-start | bytes 1622016 | tf_op jit(solution)/shard_map/all_gather | solution.py:524
  15.0 1.4 %copy-start = (bf16[2,176,2048]{2,1,0:T(8,128)(2,1)S(1)}, bf16[2,176,2048]{2,1,0:T(8,128)(2,1)}, u32[]{:S(2)}) copy-start(bf16[2,176,2048]{2,1,0:T(8,128)(2,1)} %param.17) | copy-start | bytes 4325380
  16.4 0.9 copy-start.4
  17.3 0.7 copy-start.6
  18.0 0.7 copy-start.7
  87.7 1.1 copy-start.1
  88.8 1.1 copy-start.2
  89.9 0.7 copy-start.3
  90.6 0.6 copy-start.5
Sparse Core Ops, SparseCore 0:
  10.1 49.0 all-gather.1
